TPU v7x, 128 devices: a whole 4x4x4 slice. The times are simulated.
128 devices in a mesh: packs: 8 (over x, core), seq: 16 (over y, z).
Axes of the slice: x: 4, y: 4, z: 4, core: 2. Of those that a mesh axis runs over, the one named last changes fastest.
Arguments:
- queries: bfloat16 [16384, 8192], P(('packs', 'seq')), parts along dimension 0, may hold values from -12 to 12
- keys: bfloat16 [16384, 1024], P(('packs', 'seq')), parts along dimension 0, may hold values from -6 to 6
- values: bfloat16 [16384, 1024], P(('packs', 'seq')), parts along dimension 0, may hold values from -6 to 6
- outputs: bfloat16 [16384, 8192], P(('packs', 'seq')), parts along dimension 0, may hold values from -6 to 6
- grad_out: bfloat16 [16384, 8192], P(('packs', 'seq')), parts along dimension 0, may hold values from -4 to 4
- lse_saved: float32 [16384, 64], P(('packs', 'seq')), parts along dimension 0, may hold values from -40 to 40
- doc_lengths: int32 [64], P('packs'), parts along dimension 0, may hold values from 1 to 1024, as said below
Outputs:
- grad_queries: bfloat16 [16384, 8192], P(('packs', 'seq')), parts along dimension 0
- grad_keys: bfloat16 [16384, 1024], P(('packs', 'seq')), parts along dimension 0
- grad_values: bfloat16 [16384, 1024], P(('packs', 'seq')), parts along dimension 0
There are 8 independent parts, one for each index of `packs`. A program takes and returns all parts, laid end to end along the dimension named above; each array names one. Nothing has to cross between parts.
Inputs may be any that keep to these rules, and one draw needn't show every extreme that they name: `doc_lengths`: positive lengths summing to 2048; one document has exactly 1024 tokens.
All inputs are finite; a program needn't handle non-finite values.
Results may differ from a plain program's by a relative error of at most 0.0049.
Values may be sent and summed in bfloat16 or wider, within the bound.
A program may use at most 64 MiB of HBM per device.

v0:
```python
import jax
import jax.numpy as jnp
from jax import lax
from jax.sharding import PartitionSpec as P

HEADS = 64
KVH = 8
HDIM = 128


def segment_ids(doc_lengths, total):
    boundary = jnp.cumsum(doc_lengths)
    position = jnp.arange(total, dtype=jnp.int32)
    return jnp.sum((position[:, None] >= boundary[None, :]).astype(jnp.int32), axis=1)


def left_dot(first, second):
    return lax.dot_general(
        first, second, (((0,), (0,)), ((), ())), preferred_element_type=jnp.float32
    )


def right_dot(first, second):
    return lax.dot_general(
        first, second, (((1,), (1,)), ((), ())), preferred_element_type=jnp.float32
    )


def block_terms(
    query_blk,
    gout_blk,
    lse_blk,
    delta_blk,
    query_seg,
    query_pos,
    key_blk,
    value_blk,
    key_seg,
    key_pos,
    scale,
):
    scores = right_dot(query_blk, key_blk) * scale
    visible = (key_pos[None, :] <= query_pos[:, None]) & (key_seg[None, :] == query_seg[:, None])
    attn_prob = jnp.where(visible, jnp.exp(scores - lse_blk[:, None]), 0.0)
    grad_prob = right_dot(gout_blk, value_blk)
    grad_score = (attn_prob * (grad_prob - delta_blk[:, None])).astype(jnp.bfloat16)
    prob_half = attn_prob.astype(jnp.bfloat16)
    grad_query = jnp.dot(grad_score, key_blk, preferred_element_type=jnp.float32) * scale
    grad_key = left_dot(grad_score, query_blk) * scale
    grad_value = left_dot(prob_half, gout_blk)
    return (grad_query, grad_key, grad_value)


def shards(queries, keys, values, outputs, grad_out, lse_saved, doc_lengths):
    seq_size = lax.axis_size("seq")
    local_rows = queries.shape[0]
    total = local_rows * seq_size
    head_dim = HDIM
    heads_here = HEADS // seq_size
    share_count = seq_size // KVH
    scale = 1.0 / head_dim**0.5

    def to_slots(array):
        return array.reshape(local_rows, seq_size, heads_here * head_dim)

    query_heads, out_heads, gout_heads = (
        lax.all_to_all(to_slots(queries), "seq", split_axis=1, concat_axis=0, tiled=True),
        lax.all_to_all(to_slots(outputs), "seq", split_axis=1, concat_axis=0, tiled=True),
        lax.all_to_all(to_slots(grad_out), "seq", split_axis=1, concat_axis=0, tiled=True),
    )
    lse_heads = lax.all_to_all(
        lse_saved.reshape(local_rows, seq_size, heads_here),
        "seq",
        split_axis=1,
        concat_axis=0,
        tiled=True,
    )
    out_heads = out_heads.reshape(total, heads_here, head_dim)
    gout_heads = gout_heads.reshape(total, heads_here, head_dim)
    delta_heads = jnp.einsum(
        "thd,thd->th", out_heads, gout_heads, preferred_element_type=jnp.float32
    )
    query_heads = query_heads.reshape(total, heads_here, head_dim)
    lse_heads = lse_heads.reshape(total, heads_here)
    key_slots = jnp.repeat(keys.reshape(local_rows, KVH, head_dim), share_count, axis=1)
    value_slots = jnp.repeat(values.reshape(local_rows, KVH, head_dim), share_count, axis=1)
    key_heads, value_heads = (
        lax.all_to_all(key_slots, "seq", split_axis=1, concat_axis=0, tiled=True),
        lax.all_to_all(value_slots, "seq", split_axis=1, concat_axis=0, tiled=True),
    )
    key_heads = key_heads.reshape(total, head_dim)
    value_heads = value_heads.reshape(total, head_dim)
    segment = segment_ids(doc_lengths, total)
    position = jnp.arange(total, dtype=jnp.int32)
    block = min(512, total)
    num_blocks = total // block

    def step(carry, index):
        grad_q_all, grad_k_acc, grad_v_acc = carry
        head = index // num_blocks
        start = index % num_blocks * block
        query_blk = lax.dynamic_slice(query_heads, (start, head, 0), (block, 1, head_dim)).reshape(
            block, head_dim
        )
        gout_blk = lax.dynamic_slice(gout_heads, (start, head, 0), (block, 1, head_dim)).reshape(
            block, head_dim
        )
        lse_blk = lax.dynamic_slice(lse_heads, (start, head), (block, 1)).reshape(block)
        delta_blk = lax.dynamic_slice(delta_heads, (start, head), (block, 1)).reshape(block)
        query_seg = lax.dynamic_slice_in_dim(segment, start, block)
        query_pos = lax.dynamic_slice_in_dim(position, start, block)
        grad_query, grad_key, grad_value = block_terms(
            query_blk,
            gout_blk,
            lse_blk,
            delta_blk,
            query_seg,
            query_pos,
            key_heads,
            value_heads,
            segment,
            position,
            scale,
        )
        grad_k_acc = grad_k_acc + grad_key
        grad_v_acc = grad_v_acc + grad_value
        grad_q_all = lax.dynamic_update_slice(
            grad_q_all,
            grad_query.astype(jnp.bfloat16).reshape(block, 1, head_dim),
            (start, head, 0),
        )
        return ((grad_q_all, grad_k_acc, grad_v_acc), None)

    start_carry = (
        jnp.zeros((total, heads_here, head_dim), jnp.bfloat16),
        jnp.zeros((total, head_dim), jnp.float32),
        jnp.zeros((total, head_dim), jnp.float32),
    )
    final_carry, unused = lax.scan(
        step, start_carry, jnp.arange(heads_here * num_blocks, dtype=jnp.int32)
    )
    grad_q_all, grad_k_acc, grad_v_acc = final_carry
    grad_queries = lax.all_to_all(
        grad_q_all.reshape(total, 1, heads_here * head_dim),
        "seq",
        split_axis=0,
        concat_axis=1,
        tiled=True,
    )
    grad_queries = grad_queries.reshape(local_rows, HEADS * head_dim)
    key_back, value_back = (
        lax.all_to_all(
            grad_k_acc.reshape(total, 1, head_dim), "seq", split_axis=0, concat_axis=1, tiled=True
        ),
        lax.all_to_all(
            grad_v_acc.reshape(total, 1, head_dim), "seq", split_axis=0, concat_axis=1, tiled=True
        ),
    )
    grad_keys = (
        jnp.sum(key_back.reshape(local_rows, KVH, share_count, head_dim), axis=2)
        .reshape(local_rows, KVH * head_dim)
        .astype(jnp.bfloat16)
    )
    grad_values = (
        jnp.sum(value_back.reshape(local_rows, KVH, share_count, head_dim), axis=2)
        .reshape(local_rows, KVH * head_dim)
        .astype(jnp.bfloat16)
    )
    return (grad_queries, grad_keys, grad_values)


def solution(mesh):
    placed = (
        P(("packs", "seq"), None),
        P(("packs", "seq"), None),
        P(("packs", "seq"), None),
        P(("packs", "seq"), None),
        P(("packs", "seq"), None),
        P(("packs", "seq"), None),
        P("packs"),
    )
    return jax.shard_map(
        shards,
        mesh=mesh,
        in_specs=placed,
        out_specs=(P(("packs", "seq"), None), P(("packs", "seq"), None), P(("packs", "seq"), None)),
        check_vma=False,
    )
```

profile of v0, /device:TPU:0, one launch (start us, length us, event | category | flops | bytes accessed | tf_op | source)
XLA Modules:
  0.0 481.4 jit_solution(6178511105931249375)
XLA Ops:
  0.7 8.3 %all-to-all-start.2 = ((f32[128,16,4]{0,2,1:T(4,128)}), f32[128,16,4]{0,2,1:T(4,128)S(1)}, u32[]{:S(2)}, u32[]{:S(2)}) async-start(f32[128,16,4]{0,2,1:T(4,128)} %bitcast.141), calls=%async_computation.2 | async-start | bytes 65536 | tf_op jit(solution)/shard_map/all_to_all | solution.py:71
  9.0 7.6 %all-to-all-done.2 = f32[128,16,4]{0,2,1:T(4,128)S(1)} async-done(((f32[128,16,4]{0,2,1:T(4,128)}), f32[128,16,4]{0,2,1:T(4,128)S(1)}, u32[]{:S(2)}, u32[]{:S(2)}) %all-to-all-start.2) | async-done | bytes 32800 | tf_op jit(solution)/shard_map/all_to_all | solution.py:71
  17.5 3.6 all-to-all-start.1
  23.5 7.9 %all-to-all-done.1 = bf16[128,16,128]{2,0,1:T(8,128)(2,1)S(1)} async-done(((bf16[128,16,128]{2,0,1:T(8,128)(2,1)}), bf16[128,16,128]{2,0,1:T(8,128)(2,1)S(1)}, u32[]{:S(2)}, u32[]{:S(2)}) %all-to-all-start.1) | async-done | bytes 524320 | tf_op jit(solution)/shard_map/all_to_all | solution.py:88
  31.4 3.7 all-to-all-start
  35.1 4.1 copy.71
  39.2 23.6 %all-to-all-done = bf16[128,16,512]{0,2,1:T(8,128)(2,1)S(1)} async-done(((bf16[128,16,512]{0,2,1:T(8,128)(2,1)}), bf16[128,16,512]{0,2,1:T(8,128)(2,1)S(1)}, u32[]{:S(2)}, u32[]{:S(2)}) %all-to-all-start) | async-done | bytes 2097184 | tf_op jit(solution)/shard_map/all_to_all | solution.py:67
  64.1 4.4 all-to-all-start.5
  68.6 4.1 copy.68
  72.6 23.6 %all-to-all-done.5 = bf16[128,16,512]{0,2,1:T(8,128)(2,1)} async-done(((bf16[128,16,512]{0,2,1:T(8,128)(2,1)}), bf16[128,16,512]{0,2,1:T(8,128)(2,1)}, u32[]{:S(2)}, u32[]{:S(2)}) %all-to-all-start.5) | async-done | bytes 2097184 | tf_op jit(solution)/shard_map/all_to_all | solution.py:68
  96.3 4.3 all-to-all-start.3
  100.7 27.7 %all-to-all-done.3 = bf16[128,16,512]{0,2,1:T(8,128)(2,1)S(1)} async-done(((bf16[128,16,512]{0,2,1:T(8,128)(2,1)}), bf16[128,16,512]{0,2,1:T(8,128)(2,1)S(1)}, u32[]{:S(2)}, u32[]{:S(2)}) %all-to-all-start.3) | async-done | bytes 2097184 | tf_op jit(solution)/shard_map/all_to_all | solution.py:69
  129.9 4.2 all-to-all-start.4
  134.4 4.3 copy.66
  138.7 4.2 reshape.128
  142.9 4.3 copy.72
  147.2 4.2 reshape.140
  151.4 4.3 copy.69
  155.6 4.1 reshape.135
  159.8 2.9 fusion.16
  164.3 235.0 %while.18 = (s32[]{:T(128)}, bf16[2048,4,128]{0,2,1:T(8,128)(2,1)}, f32[2048,128]{1,0:T(8,128)}, f32[2048,128]{1,0:T(8,128)S(1)}, s32[2048]{0:T(1024)S(1)}, /*in...) while((s32[]{:T(128)}, bf16[2048,4,128]{0,2,1:T(8,128)(2,1)}, ...), condition=%wide.region_3.4_spmd.clone.clone, body=%wide.region_2.3_spmd.clone.clone.sunk | while | flops 1354104832 | bytes 25862684 | solution.py:139
  175.1 2.7 fusion.47
  189.4 3.1 fusion.47
  204.1 3.1 fusion.47
  218.8 3.1 fusion.47
  233.6 3.1 fusion.47
  248.3 3.1 fusion.47
  263.0 3.1 fusion.47
  277.7 3.1 fusion.47
  292.4 3.1 fusion.47
  307.1 3.1 fusion.47
  321.8 3.1 fusion.47
  336.5 3.1 fusion.47
  351.3 3.1 fusion.47
  366.0 3.1 fusion.47
  380.7 3.1 fusion.47
  395.4 3.1 fusion.47
  399.3 21.5 %all_to_all.135 = f32[2048,1,128]{2,1,0:T(1,128)} all-to-all(f32[2048,1,128]{2,1,0:T(1,128)S(1)} %bitcast.123), channel_id=1, replica_groups=mesh['packs'=8,'seq'=16] {'seq'}, dimensions={0} | all-to-all | bytes 2097152 | tf_op jit(solution)/shard_map/all_to_all | solution.py:155
  420.8 4.0 all-to-all-start.7
  425.3 2.9 reduce.2
  428.3 2.9 copy.97
  431.1 2.8 reshape.156
  433.9 4.1 all-to-all-done.7
  438.0 3.7 all-to-all-start.6
  446.8 18.6 %all-to-all-done.6 = bf16[16,2,32768]{2,1,0:T(2,128)(2,1)S(1)} async-done(((bf16[16,2,32768]{2,1,0:T(2,128)(2,1)}), bf16[16,2,32768]{2,1,0:T(2,128)(2,1)S(1)}, u32[]{:S(2)}, u32[]{:S(2)}) %all-to-all-start.6) | async-done | bytes 2097184 | tf_op jit(solution)/shard_map/all_to_all | solution.py:143
  465.5 6.7 %reshape.157 = bf16[2048,1,512]{2,1,0:T(2,128)(2,1)} reshape(bf16[16,2,32768]{2,1,0:T(2,128)(2,1)S(1)} %all-to-all-done.6) | data formatting | bytes 4194304
  472.1 2.8 copy.92
  477.3 4.1 copy.80
  (213 shorter events, 159.0 us)
Async XLA Ops:
  0.6 8.3 %copy-start = (bf16[128,1024]{1,0:T(8,128)(2,1)S(1)}, bf16[128,1024]{1,0:T(8,128)(2,1)}, u32[]{:S(2)}) copy-start(bf16[128,1024]{1,0:T(8,128)(2,1)} %param.10) | copy-start | bytes 786436
  0.6 20.4 %copy-start.5 = (bf16[128,8192]{1,0:T(8,128)(2,1)S(1)}, bf16[128,8192]{1,0:T(8,128)(2,1)}, u32[]{:S(2)}) copy-start(bf16[128,8192]{1,0:T(8,128)(2,1)} %param.9) | copy-start | bytes 6291460
  0.7 15.9 %all-to-all-start.2 = ((f32[128,16,4]{0,2,1:T(4,128)}), f32[128,16,4]{0,2,1:T(4,128)S(1)}, u32[]{:S(2)}, u32[]{:S(2)}) async-start(f32[128,16,4]{0,2,1:T(4,128)} %bitcast.141), calls=%async_computation.2 | async-start | bytes 65536 | tf_op jit(solution)/shard_map/all_to_all | solution.py:71
  17.5 13.9 %all-to-all-start.1 = ((bf16[128,16,128]{2,0,1:T(8,128)(2,1)}), bf16[128,16,128]{2,0,1:T(8,128)(2,1)S(1)}, u32[]{:S(2)}, u32[]{:S(2)}) async-start(bf16[128,16,128]{2,0,1:T(8,128)(2,1)} %bitcast.5), calls=%async_computation.1 | async-start | bytes 1048576 | tf_op jit(solution)/shard_map/all_to_all | solution.py:88
  31.4 31.4 %all-to-all-start = ((bf16[128,16,512]{0,2,1:T(8,128)(2,1)}), bf16[128,16,512]{0,2,1:T(8,128)(2,1)S(1)}, u32[]{:S(2)}, u32[]{:S(2)}) async-start(bf16[128,16,512]{0,2,1:T(8,128)(2,1)} %bitcast.129), calls=%async_computation | async-start | bytes 4194304 | tf_op jit(solution)/shard_map/all_to_all | solution.py:67
  62.8 1.3 copy-start.2
  64.1 32.2 %all-to-all-start.5 = ((bf16[128,16,512]{0,2,1:T(8,128)(2,1)}), bf16[128,16,512]{0,2,1:T(8,128)(2,1)}, u32[]{:S(2)}, u32[]{:S(2)}) async-start(bf16[128,16,512]{0,2,1:T(8,128)(2,1)} %bitcast.130), calls=%async_computation.5 | async-start | bytes 4194304 | tf_op jit(solution)/shard_map/all_to_all | solution.py:68
  96.3 4.4 copy-start.6
  96.3 32.2 %all-to-all-start.3 = ((bf16[128,16,512]{0,2,1:T(8,128)(2,1)}), bf16[128,16,512]{0,2,1:T(8,128)(2,1)S(1)}, u32[]{:S(2)}, u32[]{:S(2)}) async-start(bf16[128,16,512]{0,2,1:T(8,128)(2,1)} %bitcast.131), calls=%async_computation.3 | async-start | bytes 4194304 | tf_op jit(solution)/shard_map/all_to_all | solution.py:69
  100.6 33.5 %copy-start.7 = (s32[8]{0:T(128)S(1)}, s32[8]{0:T(128)}, u32[]{:S(2)}) copy-start(s32[8]{0:T(128)} %param.15) | copy-start | bytes 100
  128.5 1.5 copy-start.3
  129.9 32.8 %all-to-all-start.4 = ((bf16[128,16,128]{2,0,1:T(8,128)(2,1)}), bf16[128,16,128]{2,0,1:T(8,128)(2,1)S(1)}, u32[]{:S(2)}, u32[]{:S(2)}) async-start(bf16[128,16,128]{2,0,1:T(8,128)(2,1)} %bitcast.16), calls=%async_computation.4 | async-start | bytes 1048576 | tf_op jit(solution)/shard_map/all_to_all | solution.py:89
  420.8 4.5 copy-start.4
  420.8 17.2 %all-to-all-start.7 = ((f32[2048,1,128]{2,1,0:T(1,128)}), f32[2048,1,128]{2,1,0:T(1,128)S(1)}, u32[]{:S(2)}, u32[]{:S(2)}) async-start(f32[2048,1,128]{2,1,0:T(1,128)} %bitcast.26), calls=%async_computation.7 | async-start | bytes 2097152 | tf_op jit(solution)/shard_map/all_to_all | solution.py:152
  438.0 27.4 %all-to-all-start.6 = ((bf16[16,2,32768]{2,1,0:T(2,128)(2,1)}), bf16[16,2,32768]{2,1,0:T(2,128)(2,1)S(1)}, u32[]{:S(2)}, u32[]{:S(2)}) async-start(bf16[16,2,32768]{2,1,0:T(2,128)(2,1)} %reshape.156), calls=%async_computation.6 | async-start | bytes 4194304 | tf_op jit(solution)/shard_map/all_to_all | solution.py:143
  477.3 4.1 copy-start.1
where the time goes:
time: 485 us; the launch traced here: 481 us
  matrix products  166 us (34%)
  waiting for transfers between devices  113 us (23%)
  local copies, waits for them, and re-layouts  93.8 us (19%)
  loops' own time  42.5 us (9%)
  starting transfers between devices  36.3 us (7%)
  blocking collectives  21.5 us (4%)
  other arithmetic  7.52 us (2%)
    dot_general x32, matrix products, left_dot(): lax.dot_general(first, second, (((0,), (0,)), ((), ())), preferred_elemen...  83.9 us
    dot_general x32, matrix products, right_dot(): lax.dot_general(first, second, (((1,), (1,)), ((), ())), preferred_elemen...  70.4 us
    another operation x1, loops' own time, shards(): lax.scan(step, start_carry, jnp.arange(heads_here * num_blocks, dtype=jnp...  42.5 us
    unnamed x26, local copies, waits for them, and re-layouts  34.3 us
    all_to_all x1, waiting for transfers between devices, shards(): lax.all_to_all(to_slots(grad_out), 'seq', split_axis=1, concat_axis=0, ti...  27.7 us
    all_to_all x1, waiting for transfers between devices, shards(): lax.all_to_all(to_slots(outputs), 'seq', split_axis=1, concat_axis=0, til...  23.6 us
    all_to_all x1, waiting for transfers between devices, shards(): lax.all_to_all(to_slots(queries), 'seq', split_axis=1, concat_axis=0, til...  23.6 us
    all_to_all x1, blocking collectives, shards(): lax.all_to_all(grad_v_acc.reshape(total, 1, head_dim), 'seq', split_axis=...  21.5 us
  transfers between devices with their start and end apart: 8, of which 7 were waited for; matrix products, arithmetic and copies ran while one was open for 11% of the time, Pallas kernels for 0%

commit v1 on v0

v1 whole, which is shorter than its diff:
```python
import functools

import jax
import jax.numpy as jnp
from jax import lax
from jax.experimental import pallas as pl
from jax.experimental.pallas import tpu as pltpu
from jax.sharding import PartitionSpec as P

HEADS = 64
KVH = 8
HDIM = 128
GROUP = HEADS // KVH
ROWS = 128
WIDE = GROUP * HDIM
SIDE = 4
SLOTS = 9
KEYS = SLOTS * ROWS
DOCS = 8
SCALE = 1.0 / HDIM**0.5
LOG2E = 1.4426950408889634
MESH = pl.DeviceIdType.MESH


def kernel(
    q_hbm,
    k_hbm,
    v_hbm,
    o_hbm,
    go_hbm,
    lse_ref,
    doc_ref,
    gq_hbm,
    gk_ref,
    gv_ref,
    kvw,
    part,
    own,
    outr,
    sums,
    yr,
    qb,
    gb,
    ob,
    gqb,
    qs,
    gs,
    lse_t,
    nlse,
    delta,
    bias,
    in_sem,
    kv_sem,
    out_sem,
    send_sem,
    recv_sem,
):
    me = lax.axis_index("seq")
    y, z = me // SIDE, lax.rem(me, SIDE)

    def at(dy, dz):
        return lax.rem(y + dy + SIDE, SIDE) * SIDE + lax.rem(z + dz + SIDE, SIDE)

    def remote(src, dst, kind, g, target):
        return pltpu.make_async_remote_copy(
            src_ref=src,
            dst_ref=dst,
            send_sem=send_sem.at[kind, g],
            recv_sem=recv_sem.at[kind, g],
            device_id={"seq": target},
            device_id_type=MESH,
        )

    up_first = jnp.where(z == 3, 1, 0)
    down_first = jnp.where(z == 0, 0, 1)
    relay_up = jnp.where(z == 3, 4, 3)
    relay_down = jnp.where(z == 0, 7, 8)

    def y_in(j, g):
        return remote(kvw.at[:, g, 0], kvw.at[:, g, j], j - 1, g, at(j, 0))

    def z_up(g):
        return remote(kvw.at[:, g, pl.ds(up_first, 2)], kvw.at[:, g, pl.ds(3, 2)], 2, g, at(0, 1))

    def z_down(g):
        return remote(
            kvw.at[:, g, pl.ds(down_first, 2)], kvw.at[:, g, pl.ds(7, 2)], 3, g, at(0, -1)
        )

    def far_up(g):
        return remote(kvw.at[:, g, relay_up], kvw.at[:, g, 5], 4, g, at(0, 1))

    def far_down(g):
        return remote(kvw.at[:, g, relay_down], kvw.at[:, g, 6], 5, g, at(0, -1))

    def z_out(d, g):
        return remote(part.at[:, g, pl.ds(2 * d - 2, 2)], outr.at[d - 1, :, g], 5 + d, g, at(0, -d))

    def y_out(j, g):
        return remote(sums.at[:, g, j - 1], yr.at[j - 1, :, g], 8 + j, g, at(-j, 0))

    def columns(g, width):
        return pl.ds(pl.multiple_of(g * width, width), width)

    def load_kv(n, g):
        src = (k_hbm, v_hbm)[n]
        return pltpu.make_async_copy(
            src.at[:, columns(g, HDIM)], kvw.at[n, g, 0], kv_sem.at[n, g]
        )

    def load_wide(n, g):
        src, dst = ((q_hbm, qb), (go_hbm, gb), (o_hbm, ob))[n]
        return pltpu.make_async_copy(src.at[:, columns(g, WIDE)], dst.at[g], in_sem.at[n, g])

    def store_wide(g):
        return pltpu.make_async_copy(gqb.at[g], gq_hbm.at[:, columns(g, WIDE)], out_sem.at[g])

    for g in range(KVH):
        load_kv(0, g).start()
        load_kv(1, g).start()
    for g in range(KVH):
        for n in range(3):
            load_wide(n, g).start()

    barrier = pltpu.get_barrier_semaphore()
    for dy, dz in ((1, 0), (2, 0), (3, 0), (0, 1), (0, 2), (0, 3)):
        pl.semaphore_signal(
            barrier, inc=1, device_id={"seq": at(dy, dz)}, device_id_type=MESH
        )
    pl.semaphore_wait(barrier, 6)

    for g in range(KVH):
        load_kv(0, g).wait()
        load_kv(1, g).wait()
        y_in(1, g).start()
        y_in(2, g).start()

    lse_t[...] = lse_ref[...].T * LOG2E
    time = lax.broadcasted_iota(jnp.int32, (1, ROWS), 1) + me * ROWS
    begin = jnp.zeros((1, ROWS), jnp.int32)
    bound = doc_ref[0]
    for n in range(1, DOCS):
        begin = jnp.where(time >= bound, bound, begin)
        bound = bound + doc_ref[n]
    for slot in range(SLOTS):
        if slot < 3:
            row, col = at(-slot, 0), 0
        else:
            d, second = (slot - 3) // 2 + 1, (slot - 3) % 2
            wrapped = jnp.where(z >= d, 0, 1)
            row = lax.rem(y - wrapped - second + SIDE, SIDE) * SIDE + lax.rem(z - d + SIDE, SIDE)
        keys_at = lax.broadcasted_iota(jnp.int32, (ROWS, ROWS), 0) + row * ROWS
        seen = (keys_at <= time) & (keys_at >= begin)
        bias[pl.ds(slot * ROWS, ROWS), :] = jnp.where(seen, 0.0, -1e30)

    def compute(g):
        for n in range(3):
            load_wide(n, g).wait()
        logs = lse_t[pl.ds(pl.multiple_of(g * GROUP, GROUP), GROUP), :]
        for h in range(GROUP):
            cut = slice(h * HDIM, (h + 1) * HDIM)
            query, gout = qb[g, :, cut], gb[g, :, cut]
            qs[cut, :] = query
            gs[cut, :] = gout
            product = ob[g, :, cut].astype(jnp.float32) * gout.astype(jnp.float32)
            delta[:, cut] = jnp.sum(product.T, axis=0, keepdims=True)
            nlse[:, cut] = logs[h : h + 1, :]
        k = kvw[0, g].reshape(KEYS, HDIM)
        v = kvw[1, g].reshape(KEYS, HDIM)
        nt = (((1,), (1,)), ((), ()))
        tn = (((0,), (0,)), ((), ()))
        scores = lax.dot_general(k, qs[...], nt, preferred_element_type=jnp.float32)
        hidden = jnp.concatenate([bias[...]] * GROUP, axis=1)
        prob = jnp.exp2(scores * (SCALE * LOG2E) - nlse[...] + hidden)
        grad_prob = lax.dot_general(v, gs[...], nt, preferred_element_type=jnp.float32)
        grad_score = (prob * (grad_prob - delta[...])).astype(jnp.bfloat16)
        half = prob.astype(jnp.bfloat16)
        grad_v = jnp.dot(half, gs[...], preferred_element_type=jnp.float32)
        grad_k = jnp.dot(grad_score, qs[...], preferred_element_type=jnp.float32) * SCALE
        near = 3 * ROWS
        for n, grad in ((0, grad_k), (1, grad_v)):
            own[n, g] = grad[:near].reshape(3, ROWS, HDIM)
            part[n, g] = grad[near:].reshape(6, ROWS, HDIM).astype(jnp.bfloat16)
        grad_q = lax.dot_general(k, grad_score, tn, preferred_element_type=jnp.float32)
        for h in range(GROUP):
            cut = slice(h * HDIM, (h + 1) * HDIM)
            gqb[g, :, cut] = (grad_q[:, cut].T * SCALE).astype(jnp.bfloat16)
        store_wide(g).start()

    def step(s, carry):
        @pl.when(s < KVH)
        def _():
            y_in(1, s).wait_recv()
            y_in(2, s).wait_recv()
            z_up(s).start()
            z_down(s).start()

        @pl.when((s >= 1) & (s < KVH + 1))
        def _():
            g = s - 1
            z_up(g).wait_recv()
            z_down(g).wait_recv()
            far_up(g).start()
            far_down(g).start()

        @pl.when((s >= 2) & (s < KVH + 2))
        def _():
            g = s - 2
            far_up(g).wait_recv()
            far_down(g).wait_recv()
            compute(g)
            for d in (1, 2, 3):
                z_out(d, g).start()

        @pl.when((s >= 3) & (s < KVH + 3))
        def _():
            g = s - 3
            for d in (1, 2, 3):
                z_out(d, g).wait_recv()
                first = jnp.where(z + d < SIDE, 0, 1)
                for n in range(2):
                    own[n, g, pl.ds(first, 2)] += outr[d - 1, n, g].astype(jnp.float32)
            for n in range(2):
                sums[n, g] = own[n, g, pl.ds(1, 2)].astype(jnp.bfloat16)
            y_out(1, g).start()
            y_out(2, g).start()

        @pl.when(s >= 4)
        def _():
            g = s - 4
            y_out(1, g).wait_recv()
            y_out(2, g).wait_recv()
            for n, ref in ((0, gk_ref), (1, gv_ref)):
                total = (
                    own[n, g, 0]
                    + yr[0, n, g].astype(jnp.float32)
                    + yr[1, n, g].astype(jnp.float32)
                )
                ref[:, columns(g, HDIM)] = total.astype(jnp.bfloat16)

        return carry

    lax.fori_loop(0, KVH + 4, step, 0)

    def drain(g, carry):
        y_in(1, g).wait_send()
        y_in(2, g).wait_send()
        z_up(g).wait_send()
        z_down(g).wait_send()
        far_up(g).wait_send()
        far_down(g).wait_send()
        for d in (1, 2, 3):
            z_out(d, g).wait_send()
        y_out(1, g).wait_send()
        y_out(2, g).wait_send()
        store_wide(g).wait()
        return carry

    lax.fori_loop(0, KVH, drain, 0)


def shards(queries, keys, values, outputs, grad_out, lse_saved, doc_lengths):
    half, full = jnp.bfloat16, jnp.float32
    anywhere = pl.BlockSpec(memory_space=pl.ANY)
    vmem = pl.BlockSpec(memory_space=pltpu.VMEM)
    return pl.pallas_call(
        kernel,
        out_shape=(
            jax.ShapeDtypeStruct((ROWS, HEADS * HDIM), half),
            jax.ShapeDtypeStruct((ROWS, KVH * HDIM), half),
            jax.ShapeDtypeStruct((ROWS, KVH * HDIM), half),
        ),
        in_specs=[anywhere] * 5 + [vmem, pl.BlockSpec(memory_space=pltpu.SMEM)],
        out_specs=(anywhere, vmem, vmem),
        scratch_shapes=[
            pltpu.VMEM((2, KVH, SLOTS, ROWS, HDIM), half),
            pltpu.VMEM((2, KVH, 6, ROWS, HDIM), half),
            pltpu.VMEM((2, KVH, 3, ROWS, HDIM), full),
            pltpu.VMEM((3, 2, KVH, 2, ROWS, HDIM), half),
            pltpu.VMEM((2, KVH, 2, ROWS, HDIM), half),
            pltpu.VMEM((2, 2, KVH, ROWS, HDIM), half),
            pltpu.VMEM((KVH, ROWS, WIDE), half),
            pltpu.VMEM((KVH, ROWS, WIDE), half),
            pltpu.VMEM((KVH, ROWS, WIDE), half),
            pltpu.VMEM((KVH, ROWS, WIDE), half),
            pltpu.VMEM((WIDE, HDIM), half),
            pltpu.VMEM((WIDE, HDIM), half),
            pltpu.VMEM((HEADS, ROWS), full),
            pltpu.VMEM((1, WIDE), full),
            pltpu.VMEM((1, WIDE), full),
            pltpu.VMEM((KEYS, ROWS), full),
            pltpu.SemaphoreType.DMA((3, KVH)),
            pltpu.SemaphoreType.DMA((2, KVH)),
            pltpu.SemaphoreType.DMA((KVH,)),
            pltpu.SemaphoreType.DMA((11, KVH)),
            pltpu.SemaphoreType.DMA((11, KVH)),
        ],
        compiler_params=pltpu.CompilerParams(
            collective_id=0,
            has_side_effects=True,
            vmem_limit_bytes=62 * 1024 * 1024,
        ),
        name="attention_backward",
    )(queries, keys, values, outputs, grad_out, lse_saved, doc_lengths)


def solution(mesh):
    placed = P(("packs", "seq"), None)
    return jax.shard_map(
        shards,
        mesh=mesh,
        in_specs=(placed,) * 6 + (P("packs"),),
        out_specs=(placed,) * 3,
        check_vma=False,
    )
```

time: 485 us -> 109 us (0.22)
  matrix products: 166 us -> 0 us
  waiting for transfers between devices: 113 us -> 0 us
  Pallas kernels: 0 us -> 101 us
  local copies, waits for them, and re-layouts: 93.8 us -> 6.05 us
  loops' own time: 42.5 us -> 0 us
  starting transfers between devices: 36.3 us -> 0 us
  blocking collectives: 21.5 us -> 0 us
  other arithmetic: 7.52 us -> 0 us
    dot_general x80 -> x0, matrix products: 166 us -> none  [the longest x32 83.9 us: left_dot(): lax.dot_general(first, second, (((0,), (0,)), ((), ())), preferred_elemen...]
    all_to_all x8 -> x0, waiting for transfers between devices: 113 us -> none  [the longest x1 27.7 us: shards(): lax.all_to_all(to_slots(grad_out), 'seq', split_axis=1, concat_axis=0, ti...]
    pallas_call x0 -> x1, Pallas kernels: none -> 101 us  [shards(): pl.pallas_call(kernel, out_shape=(jax.ShapeDtypeStruct((ROWS, HEADS * HDI...]
    another operation x1 -> x0, loops' own time: 42.5 us -> none  [shards(): lax.scan(step, start_carry, jnp.arange(heads_here * num_blocks, dtype=jnp...]
    all_to_all x8 -> x0, starting transfers between devices: 36.3 us -> none  [the longest x1 8.3 us: shards(): lax.all_to_all(lse_saved.reshape(local_rows, seq_size, heads_here), 'seq'...]
    unnamed x26 -> x8, local copies, waits for them, and re-layouts: 34.3 us -> 6.05 us
    all_to_all x1 -> x0, blocking collectives: 21.5 us -> none  [shards(): lax.all_to_all(grad_v_acc.reshape(total, 1, head_dim), 'seq', split_axis=...]
    all_to_all x4 -> x0, local copies, waits for them, and re-layouts: 15.2 us -> none  [the longest x1 4.3 us: shards(): lax.all_to_all(to_slots(queries), 'seq', split_axis=1, concat_axis=0, til...]
  transfers between devices with their start and end apart: 8 -> 0, of which waited for: 7 -> 0; matrix products, arithmetic and copies ran while one was open for 11% -> 0% of each run, Pallas kernels for 0% -> 0%
where the time goes in v1:
time: 109 us; the launch traced here: 108 us
  Pallas kernels  101 us (93%)
  local copies, waits for them, and re-layouts  6.05 us (6%)
    pallas_call x1, Pallas kernels, shards(): pl.pallas_call(kernel, out_shape=(jax.ShapeDtypeStruct((ROWS, HEADS * HDI...  101 us
    unnamed x8, local copies, waits for them, and re-layouts  6.05 us

profile of v1, /device:TPU:0, one launch (start us, length us, event | category | flops | bytes accessed | tf_op | source)
XLA Modules:
  0.0 107.6 jit_solution(14264000041950597851)
XLA Ops:
  0.6 1.5 %copy.10.lse_ref = f32[128,64]{1,0:T(8,128)} copy(f32[128,64]{0,1:T(8,128)} %param.12) | data formatting | bytes 65536 | tf_op args[5]
  2.1 100.9 %attention_backward.1 = (bf16[128,8192]{1,0:T(8,128)(2,1)}, bf16[128,1024]{1,0:T(8,128)(2,1)}, bf16[128,1024]{1,0:T(8,128)(2,1)}) custom-call(bf16[128,8192]{1,0:T(8,128)(2,1)} %q_hbm.1, bf16[128,1024]{1,0:T(8,128)(2,1)} %k_hbm.1, bf16[128,1024]{1,0:T(8,128)(2,1)} %v_hbm.1, bf16[128,8192]{1,0:T(8,128)(2,1)} %o_hbm.1, bf16[128,8192]{1,0:T(8,128)(2,1)} %go_hbm.1, ...), custom_call_target="tpu_custom_call" | custom-call | tf_op jit(solution)/shard_map/attention_backward/pallas_call | solution.py:266
  103.0 0.0 copy-start.1
  103.0 0.0 copy-start
  103.0 3.2 %copy.14 = bf16[128,8192]{1,0:T(8,128)(2,1)} copy(bf16[128,8192]{1,0:T(8,128)(2,1)} %get-tuple-element.6) | data formatting | bytes 4194304
  106.2 0.0 copy-done.1
  106.2 0.7 copy.15
  106.9 0.0 copy-done
  106.9 0.7 copy.16
Async XLA Ops:
  103.0 3.2 %copy-start.1 = (bf16[128,1024]{1,0:T(8,128)(2,1)S(1)}, bf16[128,1024]{1,0:T(8,128)(2,1)}, u32[]{:S(2)}) copy-start(bf16[128,1024]{1,0:T(8,128)(2,1)} %get-tuple-element.7) | copy-start | bytes 786436
  103.0 3.9 %copy-start = (bf16[128,1024]{1,0:T(8,128)(2,1)S(1)}, bf16[128,1024]{1,0:T(8,128)(2,1)}, u32[]{:S(2)}) copy-start(bf16[128,1024]{1,0:T(8,128)(2,1)} %get-tuple-element.8) | copy-start | bytes 786436

commit v2 on v1

--- a/solution.py
+++ b/solution.py
@@ -17,6 +17,7 @@
 SLOTS = 9
 KEYS = SLOTS * ROWS
 DOCS = 8
+LAG = (1, 2, 3, 4, 5)
 SCALE = 1.0 / HDIM**0.5
 LOG2E = 1.4426950408889634
 MESH = pl.DeviceIdType.MESH
@@ -35,10 +36,14 @@
     gv_ref,
     kvw,
     part,
-    own,
-    outr,
-    sums,
-    yr,
+    acc,
+    partr,
+    cross,
+    crossr,
+    side,
+    sider,
+    prev,
+    prevr,
     qb,
     gb,
     ob,
@@ -71,33 +76,36 @@
             device_id_type=MESH,
         )
 
-    up_first = jnp.where(z == 3, 1, 0)
-    down_first = jnp.where(z == 0, 0, 1)
-    relay_up = jnp.where(z == 3, 4, 3)
-    relay_down = jnp.where(z == 0, 7, 8)
+    firsts = (jnp.where(z < 3, 0, 1), jnp.where(z < 2, 0, 1), jnp.where(z < 1, 0, 1))
 
     def y_in(j, g):
-        return remote(kvw.at[:, g, 0], kvw.at[:, g, j], j - 1, g, at(j, 0))
-
-    def z_up(g):
-        return remote(kvw.at[:, g, pl.ds(up_first, 2)], kvw.at[:, g, pl.ds(3, 2)], 2, g, at(0, 1))
-
-    def z_down(g):
+        return remote(kvw.at[:, g, j - 1], kvw.at[:, g, j], j - 1, g, at(1, 0))
+
+    def z_in(d, g):
+        return remote(kvw.at[:, g, firsts[d - 1]], kvw.at[:, g, 2 + d], 1 + d, g, at(0, d))
+
+    second = firsts[0] + 1
+
+    def k_in(g):
+        return remote(kvw.at[0, g, second], kvw.at[0, g, 6], 5, g, at(0, 1))
+
+    def row_in(n, g):
         return remote(
-            kvw.at[:, g, pl.ds(down_first, 2)], kvw.at[:, g, pl.ds(7, 2)], 3, g, at(0, -1)
+            kvw.at[n, g, pl.ds(4 - n, 2 + n)], kvw.at[n, g, pl.ds(7 - n, 2 + n)], 6 + n, g, at(1, 0)
         )
 
-    def far_up(g):
-        return remote(kvw.at[:, g, relay_up], kvw.at[:, g, 5], 4, g, at(0, 1))
-
-    def far_down(g):
-        return remote(kvw.at[:, g, relay_down], kvw.at[:, g, 6], 5, g, at(0, -1))
+    def row_out(n, g):
+        rows = pl.ds(1 - n, 2 + n)
+        return remote(part.at[n, g, rows], partr.at[n, g, rows], 8 + n, g, at(-1, 0))
+
+    def k_out(g):
+        return remote(cross.at[g], crossr.at[g], 10, g, at(0, -1))
 
     def z_out(d, g):
-        return remote(part.at[:, g, pl.ds(2 * d - 2, 2)], outr.at[d - 1, :, g], 5 + d, g, at(0, -d))
+        return remote(side.at[:, g, d - 1], sider.at[d - 1, :, g], 10 + d, g, at(0, -d))
 
     def y_out(j, g):
-        return remote(sums.at[:, g, j - 1], yr.at[j - 1, :, g], 8 + j, g, at(-j, 0))
+        return remote(prev.at[:, g, j], prevr.at[:, g, j], 14 + j, g, at(-1, 0))
 
     def columns(g, width):
         return pl.ds(pl.multiple_of(g * width, width), width)
@@ -129,13 +137,15 @@
         )
     pl.semaphore_wait(barrier, 6)
 
-    for g in range(KVH):
+    def send_first(g):
         load_kv(0, g).wait()
         load_kv(1, g).wait()
         y_in(1, g).start()
-        y_in(2, g).start()
-
-    lse_t[...] = lse_ref[...].T * LOG2E
+
+    send_first(0)
+    send_first(1)
+
+    lse_t[...] = lse_ref[...] * LOG2E
     time = lax.broadcasted_iota(jnp.int32, (1, ROWS), 1) + me * ROWS
     begin = jnp.zeros((1, ROWS), jnp.int32)
     bound = doc_ref[0]
@@ -143,12 +153,8 @@
         begin = jnp.where(time >= bound, bound, begin)
         bound = bound + doc_ref[n]
     for slot in range(SLOTS):
-        if slot < 3:
-            row, col = at(-slot, 0), 0
-        else:
-            d, second = (slot - 3) // 2 + 1, (slot - 3) % 2
-            wrapped = jnp.where(z >= d, 0, 1)
-            row = lax.rem(y - wrapped - second + SIDE, SIDE) * SIDE + lax.rem(z - d + SIDE, SIDE)
+        back = (0, 4, 8, 1, 2, 3, 5, 6, 7)[slot]
+        row = lax.rem(me - back + SIDE * SIDE, SIDE * SIDE)
         keys_at = lax.broadcasted_iota(jnp.int32, (ROWS, ROWS), 0) + row * ROWS
         seen = (keys_at <= time) & (keys_at >= begin)
         bias[pl.ds(slot * ROWS, ROWS), :] = jnp.where(seen, 0.0, -1e30)
@@ -177,10 +183,11 @@
         half = prob.astype(jnp.bfloat16)
         grad_v = jnp.dot(half, gs[...], preferred_element_type=jnp.float32)
         grad_k = jnp.dot(grad_score, qs[...], preferred_element_type=jnp.float32) * SCALE
-        near = 3 * ROWS
         for n, grad in ((0, grad_k), (1, grad_v)):
-            own[n, g] = grad[:near].reshape(3, ROWS, HDIM)
-            part[n, g] = grad[near:].reshape(6, ROWS, HDIM).astype(jnp.bfloat16)
+            tile = grad.reshape(SLOTS, ROWS, HDIM)
+            acc[n, g] = tile[0:6]
+            part[n, g] = tile[6:9].astype(jnp.bfloat16)
+        cross[g] = part[0, g, 0]
         grad_q = lax.dot_general(k, grad_score, tn, preferred_element_type=jnp.float32)
         for h in range(GROUP):
             cut = slice(h * HDIM, (h + 1) * HDIM)
@@ -191,68 +198,88 @@
         @pl.when(s < KVH)
         def _():
             y_in(1, s).wait_recv()
-            y_in(2, s).wait_recv()
-            z_up(s).start()
-            z_down(s).start()
-
-        @pl.when((s >= 1) & (s < KVH + 1))
-        def _():
-            g = s - 1
-            z_up(g).wait_recv()
-            z_down(g).wait_recv()
-            far_up(g).start()
-            far_down(g).start()
-
-        @pl.when((s >= 2) & (s < KVH + 2))
-        def _():
-            g = s - 2
-            far_up(g).wait_recv()
-            far_down(g).wait_recv()
+            for d in (1, 2, 3):
+                z_in(d, s).start()
+            y_in(2, s).start()
+
+            @pl.when(s < KVH - 2)
+            def _():
+                send_first(s + 2)
+
+        @pl.when((s >= LAG[0]) & (s < KVH + LAG[0]))
+        def _():
+            g = s - LAG[0]
+            for d in (1, 2, 3):
+                z_in(d, g).wait_recv()
+            row_in(1, g).start()
+            row_in(0, g).start()
+            y_in(2, g).wait_recv()
+            k_in(g).start()
+
+        @pl.when((s >= LAG[1]) & (s < KVH + LAG[1]))
+        def _():
+            g = s - LAG[1]
+            k_in(g).wait_recv()
+            row_in(1, g).wait_recv()
+            row_in(0, g).wait_recv()
             compute(g)
-            for d in (1, 2, 3):
+            k_out(g).start()
+            row_out(0, g).start()
+            row_out(1, g).start()
+
+        @pl.when((s >= LAG[2]) & (s < KVH + LAG[2]))
+        def _():
+            g = s - LAG[2]
+            k_out(g).wait_recv()
+            acc[0, g, second] += crossr[g].astype(jnp.float32)
+            for n in range(2):
+                prev[n, g, 1] = acc[n, g, 2].astype(jnp.bfloat16)
+            y_out(1, g).start()
+            for n in range(2):
+                row_out(n, g).wait_recv()
+                rows = slice(1 - n, 3)
+                acc[n, g, 4 - n : 6] += partr[n, g, rows].astype(jnp.float32)
+                side[n, g] = acc[n, g, 3:6].astype(jnp.bfloat16)
+            for d in (2, 1, 3):
                 z_out(d, g).start()
 
-        @pl.when((s >= 3) & (s < KVH + 3))
-        def _():
-            g = s - 3
+        @pl.when((s >= LAG[3]) & (s < KVH + LAG[3]))
+        def _():
+            g = s - LAG[3]
+            y_out(1, g).wait_recv()
+            for n in range(2):
+                acc[n, g, 1] += prevr[n, g, 1].astype(jnp.float32)
             for d in (1, 2, 3):
                 z_out(d, g).wait_recv()
-                first = jnp.where(z + d < SIDE, 0, 1)
                 for n in range(2):
-                    own[n, g, pl.ds(first, 2)] += outr[d - 1, n, g].astype(jnp.float32)
+                    acc[n, g, firsts[d - 1]] += sider[d - 1, n, g].astype(jnp.float32)
             for n in range(2):
-                sums[n, g] = own[n, g, pl.ds(1, 2)].astype(jnp.bfloat16)
-            y_out(1, g).start()
-            y_out(2, g).start()
-
-        @pl.when(s >= 4)
-        def _():
-            g = s - 4
-            y_out(1, g).wait_recv()
-            y_out(2, g).wait_recv()
+                prev[n, g, 0] = acc[n, g, 1].astype(jnp.bfloat16)
+            y_out(0, g).start()
+
+        @pl.when(s >= LAG[4])
+        def _():
+            g = s - LAG[4]
+            y_out(0, g).wait_recv()
             for n, ref in ((0, gk_ref), (1, gv_ref)):
-                total = (
-                    own[n, g, 0]
-                    + yr[0, n, g].astype(jnp.float32)
-                    + yr[1, n, g].astype(jnp.float32)
-                )
+                total = acc[n, g, 0] + prevr[n, g, 0].astype(jnp.float32)
                 ref[:, columns(g, HDIM)] = total.astype(jnp.bfloat16)
 
         return carry
 
-    lax.fori_loop(0, KVH + 4, step, 0)
+    lax.fori_loop(0, KVH + LAG[4], step, 0)
 
     def drain(g, carry):
-        y_in(1, g).wait_send()
-        y_in(2, g).wait_send()
-        z_up(g).wait_send()
-        z_down(g).wait_send()
-        far_up(g).wait_send()
-        far_down(g).wait_send()
+        k_in(g).wait_send()
+        k_out(g).wait_send()
+        for n in range(2):
+            y_in(n + 1, g).wait_send()
+            row_in(n, g).wait_send()
+            row_out(n, g).wait_send()
+            y_out(n, g).wait_send()
         for d in (1, 2, 3):
+            z_in(d, g).wait_send()
             z_out(d, g).wait_send()
-        y_out(1, g).wait_send()
-        y_out(2, g).wait_send()
         store_wide(g).wait()
         return carry
 
@@ -274,11 +301,15 @@
         out_specs=(anywhere, vmem, vmem),
         scratch_shapes=[
             pltpu.VMEM((2, KVH, SLOTS, ROWS, HDIM), half),
-            pltpu.VMEM((2, KVH, 6, ROWS, HDIM), half),
-            pltpu.VMEM((2, KVH, 3, ROWS, HDIM), full),
-            pltpu.VMEM((3, 2, KVH, 2, ROWS, HDIM), half),
+            pltpu.VMEM((2, KVH, 3, ROWS, HDIM), half),
+            pltpu.VMEM((2, KVH, 6, ROWS, HDIM), full),
+            pltpu.VMEM((2, KVH, 3, ROWS, HDIM), half),
+            pltpu.VMEM((KVH, ROWS, HDIM), half),
+            pltpu.VMEM((KVH, ROWS, HDIM), half),
+            pltpu.VMEM((2, KVH, 3, ROWS, HDIM), half),
+            pltpu.VMEM((3, 2, KVH, ROWS, HDIM), half),
             pltpu.VMEM((2, KVH, 2, ROWS, HDIM), half),
-            pltpu.VMEM((2, 2, KVH, ROWS, HDIM), half),
+            pltpu.VMEM((2, KVH, 2, ROWS, HDIM), half),
             pltpu.VMEM((KVH, ROWS, WIDE), half),
             pltpu.VMEM((KVH, ROWS, WIDE), half),
             pltpu.VMEM((KVH, ROWS, WIDE), half),
@@ -292,8 +323,8 @@
             pltpu.SemaphoreType.DMA((3, KVH)),
             pltpu.SemaphoreType.DMA((2, KVH)),
             pltpu.SemaphoreType.DMA((KVH,)),
-            pltpu.SemaphoreType.DMA((11, KVH)),
-            pltpu.SemaphoreType.DMA((11, KVH)),
+            pltpu.SemaphoreType.DMA((16, KVH)),
+            pltpu.SemaphoreType.DMA((16, KVH)),
         ],
         compiler_params=pltpu.CompilerParams(
             collective_id=0,
@@ -301,7 +332,7 @@
             vmem_limit_bytes=62 * 1024 * 1024,
         ),
         name="attention_backward",
-    )(queries, keys, values, outputs, grad_out, lse_saved, doc_lengths)
+    )(queries, keys, values, outputs, grad_out, lse_saved.T, doc_lengths)
 
 
 def solution(mesh):

time: 109 us -> 93.5 us (0.86)
  Pallas kernels: 101 us -> 87.4 us
  local copies, waits for them, and re-layouts: 6.05 us -> 4.56 us
    pallas_call x1, Pallas kernels: 101 us -> 87.4 us  [shards(): pl.pallas_call(kernel, out_shape=(jax.ShapeDtypeStruct((ROWS, HEADS * HDI...]
    unnamed x8 -> x7, local copies, waits for them, and re-layouts: 6.05 us -> 4.56 us
where the time goes in v2:
time: 93.5 us; the launch traced here: 92.7 us
  Pallas kernels  87.4 us (93%)
  local copies, waits for them, and re-layouts  4.56 us (5%)
    pallas_call x1, Pallas kernels, shards(): pl.pallas_call(kernel, out_shape=(jax.ShapeDtypeStruct((ROWS, HEADS * HDI...  87.4 us
    unnamed x7, local copies, waits for them, and re-layouts  4.56 us

profile of v2, /device:TPU:0, one launch (start us, length us, event | category | flops | bytes accessed | tf_op | source)
XLA Modules:
  0.0 92.7 jit_solution(15981821016342545861)
XLA Ops:
  0.6 87.4 %attention_backward.1 = (bf16[128,8192]{1,0:T(8,128)(2,1)}, bf16[128,1024]{1,0:T(8,128)(2,1)}, bf16[128,1024]{1,0:T(8,128)(2,1)}) custom-call(bf16[128,8192]{1,0:T(8,128)(2,1)} %q_hbm.1, bf16[128,1024]{1,0:T(8,128)(2,1)} %k_hbm.1, bf16[128,1024]{1,0:T(8,128)(2,1)} %v_hbm.1, bf16[128,8192]{1,0:T(8,128)(2,1)} %o_hbm.1, bf16[128,8192]{1,0:T(8,128)(2,1)} %go_hbm.1, ...), custom_call_target="tpu_custom_call" | custom-call | tf_op jit(solution)/shard_map/attention_backward/pallas_call | solution.py:293
  88.1 0.0 copy-start.1
  88.1 0.0 copy-start
  88.1 3.2 %copy.13 = bf16[128,8192]{1,0:T(8,128)(2,1)} copy(bf16[128,8192]{1,0:T(8,128)(2,1)} %get-tuple-element.6) | data formatting | bytes 4194304
  91.3 0.0 copy-done.1
  91.3 0.7 copy.14
  92.0 0.0 copy-done
  92.0 0.7 copy.15
Async XLA Ops:
  88.1 3.2 %copy-start.1 = (bf16[128,1024]{1,0:T(8,128)(2,1)S(1)}, bf16[128,1024]{1,0:T(8,128)(2,1)}, u32[]{:S(2)}) copy-start(bf16[128,1024]{1,0:T(8,128)(2,1)} %get-tuple-element.7) | copy-start | bytes 786436
  88.1 3.9 %copy-start = (bf16[128,1024]{1,0:T(8,128)(2,1)S(1)}, bf16[128,1024]{1,0:T(8,128)(2,1)}, u32[]{:S(2)}) copy-start(bf16[128,1024]{1,0:T(8,128)(2,1)} %get-tuple-element.8) | copy-start | bytes 786436

commit v3 on v2

--- a/solution.py
+++ b/solution.py
@@ -18,6 +18,9 @@
 KEYS = SLOTS * ROWS
 DOCS = 8
 LAG = (1, 2, 3, 4, 5)
+LOOK = 3
+CROSS = ((0, 0), (0, 1))
+ROWSPAN = tuple((int((n, 0) in CROSS), 3 - int((n, 1) in CROSS)) for n in range(2))
 SCALE = 1.0 / HDIM**0.5
 LOG2E = 1.4426950408889634
 MESH = pl.DeviceIdType.MESH
@@ -38,7 +41,6 @@
     part,
     acc,
     partr,
-    cross,
     crossr,
     side,
     sider,
@@ -54,6 +56,7 @@
     nlse,
     delta,
     bias,
+    dq,
     in_sem,
     kv_sem,
     out_sem,
@@ -84,28 +87,35 @@
     def z_in(d, g):
         return remote(kvw.at[:, g, firsts[d - 1]], kvw.at[:, g, 2 + d], 1 + d, g, at(0, d))
 
-    second = firsts[0] + 1
-
-    def k_in(g):
-        return remote(kvw.at[0, g, second], kvw.at[0, g, 6], 5, g, at(0, 1))
+    seconds = (firsts[0] + 1, firsts[2] + 1)
+
+    def cross_in(n, e, g):
+        return remote(
+            kvw.at[n, g, seconds[e]], kvw.at[n, g, 6 + 2 * e], 5 + 2 * n + e, g, at(0, 1 - 2 * e)
+        )
+
+    def cross_out(n, e, g):
+        return remote(
+            part.at[n, g, 2 * e], crossr.at[n, e, g], 9 + 2 * n + e, g, at(0, 2 * e - 1)
+        )
 
     def row_in(n, g):
+        low, high = ROWSPAN[n]
+        src, dst = pl.ds(3 + low, high - low), pl.ds(6 + low, high - low)
+        return remote(kvw.at[n, g, src], kvw.at[n, g, dst], 13 + n, g, at(1, 0))
+
+    def row_out(n, g):
+        low, high = ROWSPAN[n]
+        rows = pl.ds(low, high - low)
+        return remote(part.at[n, g, rows], partr.at[n, g, rows], 15 + n, g, at(-1, 0))
+
+    def z_out(d, n, g):
         return remote(
-            kvw.at[n, g, pl.ds(4 - n, 2 + n)], kvw.at[n, g, pl.ds(7 - n, 2 + n)], 6 + n, g, at(1, 0)
-        )
-
-    def row_out(n, g):
-        rows = pl.ds(1 - n, 2 + n)
-        return remote(part.at[n, g, rows], partr.at[n, g, rows], 8 + n, g, at(-1, 0))
-
-    def k_out(g):
-        return remote(cross.at[g], crossr.at[g], 10, g, at(0, -1))
-
-    def z_out(d, g):
-        return remote(side.at[:, g, d - 1], sider.at[d - 1, :, g], 10 + d, g, at(0, -d))
-
-    def y_out(j, g):
-        return remote(prev.at[:, g, j], prevr.at[:, g, j], 14 + j, g, at(-1, 0))
+            side.at[n, g, d - 1], sider.at[d - 1, n, g], 14 + 3 * n + d + 2, g, at(0, -d)
+        )
+
+    def y_out(j, n, g):
+        return remote(prev.at[n, g, j], prevr.at[n, g, j], 23 + 2 * j + n, g, at(-1, 0))
 
     def columns(g, width):
         return pl.ds(pl.multiple_of(g * width, width), width)
@@ -142,8 +152,8 @@
         load_kv(1, g).wait()
         y_in(1, g).start()
 
-    send_first(0)
-    send_first(1)
+    for g in range(LOOK):
+        send_first(g)
 
     lse_t[...] = lse_ref[...] * LOG2E
     time = lax.broadcasted_iota(jnp.int32, (1, ROWS), 1) + me * ROWS
@@ -159,7 +169,7 @@
         seen = (keys_at <= time) & (keys_at >= begin)
         bias[pl.ds(slot * ROWS, ROWS), :] = jnp.where(seen, 0.0, -1e30)
 
-    def compute(g):
+    def prepare(g):
         for n in range(3):
             load_wide(n, g).wait()
         logs = lse_t[pl.ds(pl.multiple_of(g * GROUP, GROUP), GROUP), :]
@@ -171,27 +181,42 @@
             product = ob[g, :, cut].astype(jnp.float32) * gout.astype(jnp.float32)
             delta[:, cut] = jnp.sum(product.T, axis=0, keepdims=True)
             nlse[:, cut] = logs[h : h + 1, :]
-        k = kvw[0, g].reshape(KEYS, HDIM)
-        v = kvw[1, g].reshape(KEYS, HDIM)
+
+    def attend(g, low, high):
+        rows = (high - low) * ROWS
+        k = kvw[0, g, low:high].reshape(rows, HDIM)
+        v = kvw[1, g, low:high].reshape(rows, HDIM)
         nt = (((1,), (1,)), ((), ()))
         tn = (((0,), (0,)), ((), ()))
         scores = lax.dot_general(k, qs[...], nt, preferred_element_type=jnp.float32)
-        hidden = jnp.concatenate([bias[...]] * GROUP, axis=1)
+        hidden = jnp.concatenate([bias[low * ROWS : high * ROWS, :]] * GROUP, axis=1)
         prob = jnp.exp2(scores * (SCALE * LOG2E) - nlse[...] + hidden)
         grad_prob = lax.dot_general(v, gs[...], nt, preferred_element_type=jnp.float32)
         grad_score = (prob * (grad_prob - delta[...])).astype(jnp.bfloat16)
         half = prob.astype(jnp.bfloat16)
         grad_v = jnp.dot(half, gs[...], preferred_element_type=jnp.float32)
         grad_k = jnp.dot(grad_score, qs[...], preferred_element_type=jnp.float32) * SCALE
-        for n, grad in ((0, grad_k), (1, grad_v)):
-            tile = grad.reshape(SLOTS, ROWS, HDIM)
-            acc[n, g] = tile[0:6]
-            part[n, g] = tile[6:9].astype(jnp.bfloat16)
-        cross[g] = part[0, g, 0]
         grad_q = lax.dot_general(k, grad_score, tn, preferred_element_type=jnp.float32)
+        shape = (high - low, ROWS, HDIM)
+        return grad_q, grad_k.reshape(shape), grad_v.reshape(shape)
+
+    def near(g):
+        prepare(g)
+        grad_q, grad_k, grad_v = attend(g, 0, 6)
+        dq[...] = grad_q
+        acc[0, g] = grad_k
+        acc[1, g] = grad_v
+
+    def distant(g):
+        grad_q, grad_k, grad_v = attend(g, 6, 9)
+        part[0, g] = grad_k.astype(jnp.bfloat16)
+        part[1, g] = grad_v.astype(jnp.bfloat16)
+        dq[...] += grad_q
+
+    def finish(g):
         for h in range(GROUP):
             cut = slice(h * HDIM, (h + 1) * HDIM)
-            gqb[g, :, cut] = (grad_q[:, cut].T * SCALE).astype(jnp.bfloat16)
+            gqb[g, :, cut] = (dq[:, cut].T * SCALE).astype(jnp.bfloat16)
         store_wide(g).start()
 
     def step(s, carry):
@@ -202,66 +227,73 @@
                 z_in(d, s).start()
             y_in(2, s).start()
 
-            @pl.when(s < KVH - 2)
+            @pl.when(s < KVH - LOOK)
             def _():
-                send_first(s + 2)
+                send_first(s + LOOK)
 
         @pl.when((s >= LAG[0]) & (s < KVH + LAG[0]))
         def _():
             g = s - LAG[0]
             for d in (1, 2, 3):
                 z_in(d, g).wait_recv()
+            row_in(0, g).start()
             row_in(1, g).start()
-            row_in(0, g).start()
             y_in(2, g).wait_recv()
-            k_in(g).start()
+            for n, e in CROSS:
+                cross_in(n, e, g).start()
 
         @pl.when((s >= LAG[1]) & (s < KVH + LAG[1]))
         def _():
             g = s - LAG[1]
-            k_in(g).wait_recv()
+            for n, e in CROSS:
+                cross_in(n, e, g).wait_recv()
+            row_in(0, g).wait_recv()
             row_in(1, g).wait_recv()
-            row_in(0, g).wait_recv()
-            compute(g)
-            k_out(g).start()
+            distant(g)
+            for n, e in CROSS:
+                cross_out(n, e, g).start()
             row_out(0, g).start()
             row_out(1, g).start()
+            finish(g)
 
         @pl.when((s >= LAG[2]) & (s < KVH + LAG[2]))
         def _():
             g = s - LAG[2]
-            k_out(g).wait_recv()
-            acc[0, g, second] += crossr[g].astype(jnp.float32)
+            for n, e in CROSS:
+                cross_out(n, e, g).wait_recv()
+                acc[n, g, seconds[e]] += crossr[n, e, g].astype(jnp.float32)
             for n in range(2):
                 prev[n, g, 1] = acc[n, g, 2].astype(jnp.bfloat16)
-            y_out(1, g).start()
+                y_out(1, n, g).start()
             for n in range(2):
                 row_out(n, g).wait_recv()
-                rows = slice(1 - n, 3)
-                acc[n, g, 4 - n : 6] += partr[n, g, rows].astype(jnp.float32)
+                low, high = ROWSPAN[n]
+                acc[n, g, 3 + low : 3 + high] += partr[n, g, low:high].astype(jnp.float32)
                 side[n, g] = acc[n, g, 3:6].astype(jnp.bfloat16)
-            for d in (2, 1, 3):
-                z_out(d, g).start()
+                for d in (2, 1, 3):
+                    z_out(d, n, g).start()
+
+        @pl.when((s >= LAG[1] - 1) & (s < KVH + LAG[1] - 1))
+        def _():
+            near(s - LAG[1] + 1)
 
         @pl.when((s >= LAG[3]) & (s < KVH + LAG[3]))
         def _():
             g = s - LAG[3]
-            y_out(1, g).wait_recv()
             for n in range(2):
+                y_out(1, n, g).wait_recv()
                 acc[n, g, 1] += prevr[n, g, 1].astype(jnp.float32)
-            for d in (1, 2, 3):
-                z_out(d, g).wait_recv()
-                for n in range(2):
+                for d in (1, 3, 2):
+                    z_out(d, n, g).wait_recv()
                     acc[n, g, firsts[d - 1]] += sider[d - 1, n, g].astype(jnp.float32)
-            for n in range(2):
                 prev[n, g, 0] = acc[n, g, 1].astype(jnp.bfloat16)
-            y_out(0, g).start()
+                y_out(0, n, g).start()
 
         @pl.when(s >= LAG[4])
         def _():
             g = s - LAG[4]
-            y_out(0, g).wait_recv()
             for n, ref in ((0, gk_ref), (1, gv_ref)):
+                y_out(0, n, g).wait_recv()
                 total = acc[n, g, 0] + prevr[n, g, 0].astype(jnp.float32)
                 ref[:, columns(g, HDIM)] = total.astype(jnp.bfloat16)
 
@@ -270,27 +302,48 @@
     lax.fori_loop(0, KVH + LAG[4], step, 0)
 
     def drain(g, carry):
-        k_in(g).wait_send()
-        k_out(g).wait_send()
+        for n, e in CROSS:
+            cross_in(n, e, g).wait_send()
+            cross_out(n, e, g).wait_send()
+        for d in (1, 2, 3):
+            z_in(d, g).wait_send()
         for n in range(2):
             y_in(n + 1, g).wait_send()
             row_in(n, g).wait_send()
             row_out(n, g).wait_send()
-            y_out(n, g).wait_send()
-        for d in (1, 2, 3):
-            z_in(d, g).wait_send()
-            z_out(d, g).wait_send()
+            for j in range(2):
+                y_out(j, n, g).wait_send()
+            for d in (1, 2, 3):
+                z_out(d, n, g).wait_send()
         store_wide(g).wait()
         return carry
 
     lax.fori_loop(0, KVH, drain, 0)
+
+
+def publish(gq_in, gk_in, gv_in, gq_out, gk_out, gv_out, wide, slim, in_sem, out_sem):
+    loads, stores = [], []
+    for n in range(4):
+        rows = pl.ds(n * 32, 32)
+        loads.append(pltpu.make_async_copy(gq_in.at[rows], wide.at[rows], in_sem.at[n]))
+        stores.append(pltpu.make_async_copy(wide.at[rows], gq_out.at[rows], out_sem.at[n]))
+    for n, (src, dst) in enumerate(((gk_in, gk_out), (gv_in, gv_out))):
+        loads.append(pltpu.make_async_copy(src, slim.at[n], in_sem.at[4 + n]))
+        stores.append(pltpu.make_async_copy(slim.at[n], dst, out_sem.at[4 + n]))
+    for load in loads:
+        load.start()
+    for load, store in zip(loads, stores):
+        load.wait()
+        store.start()
+    for store in stores:
+        store.wait()
 
 
 def shards(queries, keys, values, outputs, grad_out, lse_saved, doc_lengths):
     half, full = jnp.bfloat16, jnp.float32
     anywhere = pl.BlockSpec(memory_space=pl.ANY)
     vmem = pl.BlockSpec(memory_space=pltpu.VMEM)
-    return pl.pallas_call(
+    grads = pl.pallas_call(
         kernel,
         out_shape=(
             jax.ShapeDtypeStruct((ROWS, HEADS * HDIM), half),
@@ -304,8 +357,7 @@
             pltpu.VMEM((2, KVH, 3, ROWS, HDIM), half),
             pltpu.VMEM((2, KVH, 6, ROWS, HDIM), full),
             pltpu.VMEM((2, KVH, 3, ROWS, HDIM), half),
-            pltpu.VMEM((KVH, ROWS, HDIM), half),
-            pltpu.VMEM((KVH, ROWS, HDIM), half),
+            pltpu.VMEM((2, 2, KVH, ROWS, HDIM), half),
             pltpu.VMEM((2, KVH, 3, ROWS, HDIM), half),
             pltpu.VMEM((3, 2, KVH, ROWS, HDIM), half),
             pltpu.VMEM((2, KVH, 2, ROWS, HDIM), half),
@@ -320,11 +372,12 @@
             pltpu.VMEM((1, WIDE), full),
             pltpu.VMEM((1, WIDE), full),
             pltpu.VMEM((KEYS, ROWS), full),
+            pltpu.VMEM((HDIM, WIDE), full),
             pltpu.SemaphoreType.DMA((3, KVH)),
             pltpu.SemaphoreType.DMA((2, KVH)),
             pltpu.SemaphoreType.DMA((KVH,)),
-            pltpu.SemaphoreType.DMA((16, KVH)),
-            pltpu.SemaphoreType.DMA((16, KVH)),
+            pltpu.SemaphoreType.DMA((27, KVH)),
+            pltpu.SemaphoreType.DMA((27, KVH)),
         ],
         compiler_params=pltpu.CompilerParams(
             collective_id=0,
@@ -333,6 +386,23 @@
         ),
         name="attention_backward",
     )(queries, keys, values, outputs, grad_out, lse_saved.T, doc_lengths)
+    return pl.pallas_call(
+        publish,
+        out_shape=(
+            jax.ShapeDtypeStruct((ROWS, HEADS * HDIM), half),
+            jax.ShapeDtypeStruct((ROWS, KVH * HDIM), half),
+            jax.ShapeDtypeStruct((ROWS, KVH * HDIM), half),
+        ),
+        in_specs=[anywhere] * 3,
+        out_specs=(anywhere,) * 3,
+        scratch_shapes=[
+            pltpu.VMEM((ROWS, HEADS * HDIM), half),
+            pltpu.VMEM((2, ROWS, KVH * HDIM), half),
+            pltpu.SemaphoreType.DMA((6,)),
+            pltpu.SemaphoreType.DMA((6,)),
+        ],
+        name="publish",
+    )(*grads)
 
 
 def solution(mesh):

time: 93.5 us -> 86.8 us (0.928)
  local copies, waits for them, and re-layouts: 4.56 us -> 0 us
  Pallas kernels: 87.4 us -> 85.9 us
    unnamed x7 -> x0, local copies, waits for them, and re-layouts: 4.56 us -> none
    pallas_call x1, Pallas kernels: 87.4 us -> 83.3 us  [shards(): pl.pallas_call(kernel, out_shape=(jax.ShapeDtypeStruct((ROWS, HEADS * HDI...]
    pallas_call x0 -> x1, Pallas kernels: none -> 2.63 us  [shards(): pl.pallas_call(publish, out_shape=(jax.ShapeDtypeStruct((ROWS, HEADS * HD...]
where the time goes in v3:
time: 86.8 us; the launch traced here: 86.6 us
  Pallas kernels  85.9 us (99%)
    pallas_call x1, Pallas kernels, shards(): pl.pallas_call(kernel, out_shape=(jax.ShapeDtypeStruct((ROWS, HEADS * HDI...  83.3 us
    pallas_call x1, Pallas kernels, shards(): pl.pallas_call(publish, out_shape=(jax.ShapeDtypeStruct((ROWS, HEADS * HD...  2.63 us

profile of v3, /device:TPU:0, one launch (start us, length us, event | category | flops | bytes accessed | tf_op | source)
XLA Modules:
  0.0 86.6 jit_solution(14808952589567643821)
XLA Ops:
  0.6 83.3 %attention_backward.1 = (bf16[128,8192]{1,0:T(8,128)(2,1)}, bf16[128,1024]{1,0:T(8,128)(2,1)}, bf16[128,1024]{1,0:T(8,128)(2,1)}) custom-call(bf16[128,8192]{1,0:T(8,128)(2,1)} %q_hbm.1, bf16[128,1024]{1,0:T(8,128)(2,1)} %k_hbm.1, bf16[128,1024]{1,0:T(8,128)(2,1)} %v_hbm.1, bf16[128,8192]{1,0:T(8,128)(2,1)} %o_hbm.1, bf16[128,8192]{1,0:T(8,128)(2,1)} %go_hbm.1, ...), custom_call_target="tpu_custom_call" | custom-call | tf_op jit(solution)/shard_map/attention_backward/pallas_call | solution.py:346
  83.9 2.6 %publish.1 = (bf16[128,8192]{1,0:T(8,128)(2,1)}, bf16[128,1024]{1,0:T(8,128)(2,1)}, bf16[128,1024]{1,0:T(8,128)(2,1)}) custom-call(bf16[128,8192]{1,0:T(8,128)(2,1)} %get-tuple-element.6.gq_in, bf16[128,1024]{1,0:T(8,128)(2,1)} %get-tuple-element.7.gk_in, bf16[128,1024]{1,0:T(8,128)(2,1)} %get-tuple-element.8.gv_in), custom_call_target="tpu_custom_call" | custom-call | tf_op jit(solution)/shard_map/publish/pallas_call | solution.py:389

commit v4 on v3

--- a/solution.py
+++ b/solution.py
@@ -19,8 +19,10 @@
 DOCS = 8
 LAG = (1, 2, 3, 4, 5)
 LOOK = 3
-CROSS = ((0, 0), (0, 1))
-ROWSPAN = tuple((int((n, 0) in CROSS), 3 - int((n, 1) in CROSS)) for n in range(2))
+HEAVY = ((0, 0), (0, 1), (1, 0), (1, 1))
+LIGHT = ((0, 0),)
+LEAD = 2
+TAIL = 2
 SCALE = 1.0 / HDIM**0.5
 LOG2E = 1.4426950408889634
 MESH = pl.DeviceIdType.MESH
@@ -35,8 +37,8 @@
     lse_ref,
     doc_ref,
     gq_hbm,
-    gk_ref,
-    gv_ref,
+    gk_hbm,
+    gv_hbm,
     kvw,
     part,
     acc,
@@ -57,9 +59,11 @@
     delta,
     bias,
     dq,
+    slim,
     in_sem,
     kv_sem,
     out_sem,
+    slim_sem,
     send_sem,
     recv_sem,
 ):
@@ -99,15 +103,33 @@
             part.at[n, g, 2 * e], crossr.at[n, e, g], 9 + 2 * n + e, g, at(0, 2 * e - 1)
         )
 
-    def row_in(n, g):
-        low, high = ROWSPAN[n]
+    def span(n, cross):
+        return int((n, 0) in cross), 3 - int((n, 1) in cross)
+
+    def row_in(n, cross, g):
+        low, high = span(n, cross)
         src, dst = pl.ds(3 + low, high - low), pl.ds(6 + low, high - low)
         return remote(kvw.at[n, g, src], kvw.at[n, g, dst], 13 + n, g, at(1, 0))
 
-    def row_out(n, g):
-        low, high = ROWSPAN[n]
+    def row_out(n, cross, g):
+        low, high = span(n, cross)
         rows = pl.ds(low, high - low)
         return remote(part.at[n, g, rows], partr.at[n, g, rows], 15 + n, g, at(-1, 0))
+
+    def by_load(heavy, body):
+        @pl.when(heavy)
+        def _():
+            body(HEAVY)
+
+        @pl.when(jnp.logical_not(heavy))
+        def _():
+            body(LIGHT)
+
+    def in_load(g, body):
+        by_load(g < LEAD, body)
+
+    def out_load(g, body):
+        by_load(g >= KVH - TAIL, body)
 
     def z_out(d, n, g):
         return remote(
@@ -129,6 +151,10 @@
     def load_wide(n, g):
         src, dst = ((q_hbm, qb), (go_hbm, gb), (o_hbm, ob))[n]
         return pltpu.make_async_copy(src.at[:, columns(g, WIDE)], dst.at[g], in_sem.at[n, g])
+
+    def store_slim(n, g):
+        dst = (gk_hbm, gv_hbm)[n]
+        return pltpu.make_async_copy(slim.at[n, g], dst.at[:, columns(g, HDIM)], slim_sem.at[n, g])
 
     def store_wide(g):
         return pltpu.make_async_copy(gqb.at[g], gq_hbm.at[:, columns(g, WIDE)], out_sem.at[g])
@@ -236,42 +262,57 @@
             g = s - LAG[0]
             for d in (1, 2, 3):
                 z_in(d, g).wait_recv()
-            row_in(0, g).start()
-            row_in(1, g).start()
-            y_in(2, g).wait_recv()
-            for n, e in CROSS:
-                cross_in(n, e, g).start()
+
+            def send(cross):
+                row_in(0, cross, g).start()
+                row_in(1, cross, g).start()
+                y_in(2, g).wait_recv()
+                for n, e in cross:
+                    cross_in(n, e, g).start()
+
+            in_load(g, send)
 
         @pl.when((s >= LAG[1]) & (s < KVH + LAG[1]))
         def _():
             g = s - LAG[1]
-            for n, e in CROSS:
-                cross_in(n, e, g).wait_recv()
-            row_in(0, g).wait_recv()
-            row_in(1, g).wait_recv()
+
+            def arrive(cross):
+                for n, e in cross:
+                    cross_in(n, e, g).wait_recv()
+                for n in range(2):
+                    row_in(n, cross, g).wait_recv()
+
+            def leave(cross):
+                for n, e in cross:
+                    cross_out(n, e, g).start()
+                for n in range(2):
+                    row_out(n, cross, g).start()
+
+            in_load(g, arrive)
             distant(g)
-            for n, e in CROSS:
-                cross_out(n, e, g).start()
-            row_out(0, g).start()
-            row_out(1, g).start()
+            out_load(g, leave)
             finish(g)
 
         @pl.when((s >= LAG[2]) & (s < KVH + LAG[2]))
         def _():
             g = s - LAG[2]
-            for n, e in CROSS:
-                cross_out(n, e, g).wait_recv()
-                acc[n, g, seconds[e]] += crossr[n, e, g].astype(jnp.float32)
-            for n in range(2):
-                prev[n, g, 1] = acc[n, g, 2].astype(jnp.bfloat16)
-                y_out(1, n, g).start()
-            for n in range(2):
-                row_out(n, g).wait_recv()
-                low, high = ROWSPAN[n]
-                acc[n, g, 3 + low : 3 + high] += partr[n, g, low:high].astype(jnp.float32)
-                side[n, g] = acc[n, g, 3:6].astype(jnp.bfloat16)
-                for d in (2, 1, 3):
-                    z_out(d, n, g).start()
+
+            def collect(cross):
+                for n, e in cross:
+                    cross_out(n, e, g).wait_recv()
+                    acc[n, g, seconds[e]] += crossr[n, e, g].astype(jnp.float32)
+                for n in range(2):
+                    prev[n, g, 1] = acc[n, g, 2].astype(jnp.bfloat16)
+                    y_out(1, n, g).start()
+                for n in range(2):
+                    row_out(n, cross, g).wait_recv()
+                    low, high = span(n, cross)
+                    acc[n, g, 3 + low : 3 + high] += partr[n, g, low:high].astype(jnp.float32)
+                    side[n, g] = acc[n, g, 3:6].astype(jnp.bfloat16)
+                    for d in (2, 1, 3):
+                        z_out(d, n, g).start()
+
+            out_load(g, collect)
 
         @pl.when((s >= LAG[1] - 1) & (s < KVH + LAG[1] - 1))
         def _():
@@ -292,30 +333,42 @@
         @pl.when(s >= LAG[4])
         def _():
             g = s - LAG[4]
-            for n, ref in ((0, gk_ref), (1, gv_ref)):
+            for n in range(2):
                 y_out(0, n, g).wait_recv()
                 total = acc[n, g, 0] + prevr[n, g, 0].astype(jnp.float32)
-                ref[:, columns(g, HDIM)] = total.astype(jnp.bfloat16)
+                slim[n, g] = total.astype(jnp.bfloat16)
+                store_slim(n, g).start()
 
         return carry
 
     lax.fori_loop(0, KVH + LAG[4], step, 0)
 
     def drain(g, carry):
-        for n, e in CROSS:
-            cross_in(n, e, g).wait_send()
-            cross_out(n, e, g).wait_send()
+        def sent_in(cross):
+            for n, e in cross:
+                cross_in(n, e, g).wait_send()
+            for n in range(2):
+                row_in(n, cross, g).wait_send()
+
+        def sent_out(cross):
+            for n, e in cross:
+                cross_out(n, e, g).wait_send()
+            for n in range(2):
+                row_out(n, cross, g).wait_send()
+
+        in_load(g, sent_in)
+        out_load(g, sent_out)
         for d in (1, 2, 3):
             z_in(d, g).wait_send()
         for n in range(2):
             y_in(n + 1, g).wait_send()
-            row_in(n, g).wait_send()
-            row_out(n, g).wait_send()
             for j in range(2):
                 y_out(j, n, g).wait_send()
             for d in (1, 2, 3):
                 z_out(d, n, g).wait_send()
         store_wide(g).wait()
+        store_slim(0, g).wait()
+        store_slim(1, g).wait()
         return carry
 
     lax.fori_loop(0, KVH, drain, 0)
@@ -323,13 +376,13 @@
 
 def publish(gq_in, gk_in, gv_in, gq_out, gk_out, gv_out, wide, slim, in_sem, out_sem):
     loads, stores = [], []
-    for n in range(4):
-        rows = pl.ds(n * 32, 32)
+    for n in range(8):
+        rows = pl.ds(n * 16, 16)
         loads.append(pltpu.make_async_copy(gq_in.at[rows], wide.at[rows], in_sem.at[n]))
         stores.append(pltpu.make_async_copy(wide.at[rows], gq_out.at[rows], out_sem.at[n]))
     for n, (src, dst) in enumerate(((gk_in, gk_out), (gv_in, gv_out))):
-        loads.append(pltpu.make_async_copy(src, slim.at[n], in_sem.at[4 + n]))
-        stores.append(pltpu.make_async_copy(slim.at[n], dst, out_sem.at[4 + n]))
+        loads.append(pltpu.make_async_copy(src, slim.at[n], in_sem.at[8 + n]))
+        stores.append(pltpu.make_async_copy(slim.at[n], dst, out_sem.at[8 + n]))
     for load in loads:
         load.start()
     for load, store in zip(loads, stores):
@@ -351,7 +404,7 @@
             jax.ShapeDtypeStruct((ROWS, KVH * HDIM), half),
         ),
         in_specs=[anywhere] * 5 + [vmem, pl.BlockSpec(memory_space=pltpu.SMEM)],
-        out_specs=(anywhere, vmem, vmem),
+        out_specs=(anywhere,) * 3,
         scratch_shapes=[
             pltpu.VMEM((2, KVH, SLOTS, ROWS, HDIM), half),
             pltpu.VMEM((2, KVH, 3, ROWS, HDIM), half),
@@ -373,9 +426,11 @@
             pltpu.VMEM((1, WIDE), full),
             pltpu.VMEM((KEYS, ROWS), full),
             pltpu.VMEM((HDIM, WIDE), full),
+            pltpu.VMEM((2, KVH, ROWS, HDIM), half),
             pltpu.SemaphoreType.DMA((3, KVH)),
             pltpu.SemaphoreType.DMA((2, KVH)),
             pltpu.SemaphoreType.DMA((KVH,)),
+            pltpu.SemaphoreType.DMA((2, KVH)),
             pltpu.SemaphoreType.DMA((27, KVH)),
             pltpu.SemaphoreType.DMA((27, KVH)),
         ],
@@ -398,8 +453,8 @@
         scratch_shapes=[
             pltpu.VMEM((ROWS, HEADS * HDIM), half),
             pltpu.VMEM((2, ROWS, KVH * HDIM), half),
-            pltpu.SemaphoreType.DMA((6,)),
-            pltpu.SemaphoreType.DMA((6,)),
+            pltpu.SemaphoreType.DMA((10,)),
+            pltpu.SemaphoreType.DMA((10,)),
         ],
         name="publish",
     )(*grads)

time: 86.8 us -> 82.7 us (0.953)
  Pallas kernels: 85.9 us -> 81.8 us
    pallas_call x1, Pallas kernels: 83.3 us -> 79.2 us  [shards(): pl.pallas_call(kernel, out_shape=(jax.ShapeDtypeStruct((ROWS, HEADS * HDI...]
where the time goes in v4:
time: 82.7 us; the launch traced here: 82.5 us
  Pallas kernels  81.8 us (99%)
    pallas_call x1, Pallas kernels, shards(): pl.pallas_call(kernel, out_shape=(jax.ShapeDtypeStruct((ROWS, HEADS * HDI...  79.2 us
    pallas_call x1, Pallas kernels, shards(): pl.pallas_call(publish, out_shape=(jax.ShapeDtypeStruct((ROWS, HEADS * HD...  2.6 us

profile of v4, /device:TPU:0, one launch (start us, length us, event | category | flops | bytes accessed | tf_op | source)
XLA Modules:
  0.0 82.5 jit_solution(2502879406374476646)
XLA Ops:
  0.6 79.2 %attention_backward.1 = (bf16[128,8192]{1,0:T(8,128)(2,1)}, bf16[128,1024]{1,0:T(8,128)(2,1)}, bf16[128,1024]{1,0:T(8,128)(2,1)}) custom-call(bf16[128,8192]{1,0:T(8,128)(2,1)} %q_hbm.1, bf16[128,1024]{1,0:T(8,128)(2,1)} %k_hbm.1, bf16[128,1024]{1,0:T(8,128)(2,1)} %v_hbm.1, bf16[128,8192]{1,0:T(8,128)(2,1)} %o_hbm.1, bf16[128,8192]{1,0:T(8,128)(2,1)} %go_hbm.1, ...), custom_call_target="tpu_custom_call" | custom-call | tf_op jit(solution)/shard_map/attention_backward/pallas_call | solution.py:399
  79.9 2.6 %publish.1 = (bf16[128,8192]{1,0:T(8,128)(2,1)}, bf16[128,1024]{1,0:T(8,128)(2,1)}, bf16[128,1024]{1,0:T(8,128)(2,1)}) custom-call(bf16[128,8192]{1,0:T(8,128)(2,1)} %get-tuple-element.6.gq_in, bf16[128,1024]{1,0:T(8,128)(2,1)} %get-tuple-element.7.gk_in, bf16[128,1024]{1,0:T(8,128)(2,1)} %get-tuple-element.8.gv_in), custom_call_target="tpu_custom_call" | custom-call | tf_op jit(solution)/shard_map/publish/pallas_call | solution.py:444

commit v5 on v4

--- a/solution.py
+++ b/solution.py
@@ -227,17 +227,35 @@
         return grad_q, grad_k.reshape(shape), grad_v.reshape(shape)
 
     def near(g):
-        prepare(g)
+        @pl.when(g > 0)
+        def _():
+            prepare(g)
+
         grad_q, grad_k, grad_v = attend(g, 0, 6)
         dq[...] = grad_q
         acc[0, g] = grad_k
         acc[1, g] = grad_v
 
-    def distant(g):
-        grad_q, grad_k, grad_v = attend(g, 6, 9)
-        part[0, g] = grad_k.astype(jnp.bfloat16)
-        part[1, g] = grad_v.astype(jnp.bfloat16)
-        dq[...] += grad_q
+    def distant(g, leave):
+        rows = 3 * ROWS
+        k = kvw[0, g, 6:9].reshape(rows, HDIM)
+        v = kvw[1, g, 6:9].reshape(rows, HDIM)
+        nt = (((1,), (1,)), ((), ()))
+        tn = (((0,), (0,)), ((), ()))
+        shape = (3, ROWS, HDIM)
+        scores = lax.dot_general(k, qs[...], nt, preferred_element_type=jnp.float32)
+        hidden = jnp.concatenate([bias[6 * ROWS :, :]] * GROUP, axis=1)
+        prob = jnp.exp2(scores * (SCALE * LOG2E) - nlse[...] + hidden)
+        half = prob.astype(jnp.bfloat16)
+        grad_v = jnp.dot(half, gs[...], preferred_element_type=jnp.float32)
+        part[1, g] = grad_v.reshape(shape).astype(jnp.bfloat16)
+        leave(1)
+        grad_prob = lax.dot_general(v, gs[...], nt, preferred_element_type=jnp.float32)
+        grad_score = (prob * (grad_prob - delta[...])).astype(jnp.bfloat16)
+        grad_k = jnp.dot(grad_score, qs[...], preferred_element_type=jnp.float32) * SCALE
+        part[0, g] = grad_k.reshape(shape).astype(jnp.bfloat16)
+        leave(0)
+        dq[...] += lax.dot_general(k, grad_score, tn, preferred_element_type=jnp.float32)
 
     def finish(g):
         for h in range(GROUP):
@@ -282,29 +300,30 @@
                 for n in range(2):
                     row_in(n, cross, g).wait_recv()
 
-            def leave(cross):
-                for n, e in cross:
-                    cross_out(n, e, g).start()
-                for n in range(2):
+            def leave(n):
+                def send(cross):
+                    for m, e in cross:
+                        if m == n:
+                            cross_out(n, e, g).start()
                     row_out(n, cross, g).start()
 
+                out_load(g, send)
+
             in_load(g, arrive)
-            distant(g)
-            out_load(g, leave)
-            finish(g)
+            distant(g, leave)
 
         @pl.when((s >= LAG[2]) & (s < KVH + LAG[2]))
         def _():
             g = s - LAG[2]
 
             def collect(cross):
-                for n, e in cross:
-                    cross_out(n, e, g).wait_recv()
-                    acc[n, g, seconds[e]] += crossr[n, e, g].astype(jnp.float32)
-                for n in range(2):
+                for n in (1, 0):
+                    for m, e in cross:
+                        if m == n:
+                            cross_out(n, e, g).wait_recv()
+                            acc[n, g, seconds[e]] += crossr[n, e, g].astype(jnp.float32)
                     prev[n, g, 1] = acc[n, g, 2].astype(jnp.bfloat16)
                     y_out(1, n, g).start()
-                for n in range(2):
                     row_out(n, cross, g).wait_recv()
                     low, high = span(n, cross)
                     acc[n, g, 3 + low : 3 + high] += partr[n, g, low:high].astype(jnp.float32)
@@ -314,6 +333,10 @@
 
             out_load(g, collect)
 
+        @pl.when((s >= LAG[1]) & (s < KVH + LAG[1]))
+        def _():
+            finish(s - LAG[1])
+
         @pl.when((s >= LAG[1] - 1) & (s < KVH + LAG[1] - 1))
         def _():
             near(s - LAG[1] + 1)
@@ -321,7 +344,7 @@
         @pl.when((s >= LAG[3]) & (s < KVH + LAG[3]))
         def _():
             g = s - LAG[3]
-            for n in range(2):
+            for n in (1, 0):
                 y_out(1, n, g).wait_recv()
                 acc[n, g, 1] += prevr[n, g, 1].astype(jnp.float32)
                 for d in (1, 3, 2):
@@ -341,6 +364,7 @@
 
         return carry
 
+    prepare(0)
     lax.fori_loop(0, KVH + LAG[4], step, 0)
 
     def drain(g, carry):

time: 82.7 us -> 81.7 us (0.988)
  Pallas kernels: 81.8 us -> 80.8 us
    pallas_call x1, Pallas kernels: 79.2 us -> 78.2 us  [shards(): pl.pallas_call(kernel, out_shape=(jax.ShapeDtypeStruct((ROWS, HEADS * HDI...]
where the time goes in v5:
time: 81.7 us; the launch traced here: 81.5 us
  Pallas kernels  80.8 us (99%)
    pallas_call x1, Pallas kernels, shards(): pl.pallas_call(kernel, out_shape=(jax.ShapeDtypeStruct((ROWS, HEADS * HDI...  78.2 us
    pallas_call x1, Pallas kernels, shards(): pl.pallas_call(publish, out_shape=(jax.ShapeDtypeStruct((ROWS, HEADS * HD...  2.6 us

profile of v5, /device:TPU:0, one launch (start us, length us, event | category | flops | bytes accessed | tf_op | source)
XLA Modules:
  0.0 81.5 jit_solution(12947432637464581653)
XLA Ops:
  0.6 78.2 %attention_backward.1 = (bf16[128,8192]{1,0:T(8,128)(2,1)}, bf16[128,1024]{1,0:T(8,128)(2,1)}, bf16[128,1024]{1,0:T(8,128)(2,1)}) custom-call(bf16[128,8192]{1,0:T(8,128)(2,1)} %q_hbm.1, bf16[128,1024]{1,0:T(8,128)(2,1)} %k_hbm.1, bf16[128,1024]{1,0:T(8,128)(2,1)} %v_hbm.1, bf16[128,8192]{1,0:T(8,128)(2,1)} %o_hbm.1, bf16[128,8192]{1,0:T(8,128)(2,1)} %go_hbm.1, ...), custom_call_target="tpu_custom_call" | custom-call | tf_op jit(solution)/shard_map/attention_backward/pallas_call | solution.py:423
  78.9 2.6 %publish.1 = (bf16[128,8192]{1,0:T(8,128)(2,1)}, bf16[128,1024]{1,0:T(8,128)(2,1)}, bf16[128,1024]{1,0:T(8,128)(2,1)}) custom-call(bf16[128,8192]{1,0:T(8,128)(2,1)} %get-tuple-element.6.gq_in, bf16[128,1024]{1,0:T(8,128)(2,1)} %get-tuple-element.7.gk_in, bf16[128,1024]{1,0:T(8,128)(2,1)} %get-tuple-element.8.gv_in), custom_call_target="tpu_custom_call" | custom-call | tf_op jit(solution)/shard_map/publish/pallas_call | solution.py:468

commit v6 on v5

--- a/solution.py
+++ b/solution.py
@@ -267,9 +267,9 @@
         @pl.when(s < KVH)
         def _():
             y_in(1, s).wait_recv()
-            for d in (1, 2, 3):
+            y_in(2, s).start()
+            for d in (2, 1, 3):
                 z_in(d, s).start()
-            y_in(2, s).start()
 
             @pl.when(s < KVH - LOOK)
             def _():
@@ -278,15 +278,15 @@
         @pl.when((s >= LAG[0]) & (s < KVH + LAG[0]))
         def _():
             g = s - LAG[0]
-            for d in (1, 2, 3):
-                z_in(d, g).wait_recv()
+            y_in(2, g).wait_recv()
 
             def send(cross):
+                for n, e in cross:
+                    cross_in(n, e, g).start()
+                for d in (1, 3, 2):
+                    z_in(d, g).wait_recv()
                 row_in(0, cross, g).start()
                 row_in(1, cross, g).start()
-                y_in(2, g).wait_recv()
-                for n, e in cross:
-                    cross_in(n, e, g).start()
 
             in_load(g, send)
 

time: 81.7 us -> 81.7 us (level)
  no operation moved by 1% of the time
where the time goes in v6:
time: 81.7 us; the launch traced here: 81.5 us
  Pallas kernels  80.9 us (99%)
    pallas_call x1, Pallas kernels, shards(): pl.pallas_call(kernel, out_shape=(jax.ShapeDtypeStruct((ROWS, HEADS * HDI...  78.3 us
    pallas_call x1, Pallas kernels, shards(): pl.pallas_call(publish, out_shape=(jax.ShapeDtypeStruct((ROWS, HEADS * HD...  2.6 us

profile of v6, /device:TPU:0, one launch (start us, length us, event | category | flops | bytes accessed | tf_op | source)
XLA Modules:
  0.0 81.5 jit_solution(16442455100841336468)
XLA Ops:
  0.6 78.3 %attention_backward.1 = (bf16[128,8192]{1,0:T(8,128)(2,1)}, bf16[128,1024]{1,0:T(8,128)(2,1)}, bf16[128,1024]{1,0:T(8,128)(2,1)}) custom-call(bf16[128,8192]{1,0:T(8,128)(2,1)} %q_hbm.1, bf16[128,1024]{1,0:T(8,128)(2,1)} %k_hbm.1, bf16[128,1024]{1,0:T(8,128)(2,1)} %v_hbm.1, bf16[128,8192]{1,0:T(8,128)(2,1)} %o_hbm.1, bf16[128,8192]{1,0:T(8,128)(2,1)} %go_hbm.1, ...), custom_call_target="tpu_custom_call" | custom-call | tf_op jit(solution)/shard_map/attention_backward/pallas_call | solution.py:423
  78.9 2.6 %publish.1 = (bf16[128,8192]{1,0:T(8,128)(2,1)}, bf16[128,1024]{1,0:T(8,128)(2,1)}, bf16[128,1024]{1,0:T(8,128)(2,1)}) custom-call(bf16[128,8192]{1,0:T(8,128)(2,1)} %get-tuple-element.6.gq_in, bf16[128,1024]{1,0:T(8,128)(2,1)} %get-tuple-element.7.gk_in, bf16[128,1024]{1,0:T(8,128)(2,1)} %get-tuple-element.8.gv_in), custom_call_target="tpu_custom_call" | custom-call | tf_op jit(solution)/shard_map/publish/pallas_call | solution.py:468
